TPU v7x, 32 devices: a whole 2x2x4 slice. The times are simulated.
32 devices in a mesh: ctx: 8 (over z, y), dp: 4 (over x, core).
Axes of the slice: x: 2, y: 2, z: 4, core: 2. Of those that a mesh axis runs over, the one named last changes fastest.
Arguments:
- tokens: bfloat16 [4, 4096, 768], P('dp', 'ctx'), may hold values from -6 to 6
- cotangent: bfloat16 [4, 4096, 768], P('dp', 'ctx'), may hold values from -6 to 6
- attn_gain: bfloat16 [768], P('dp'), may hold values from 0.099609375 to 1.8984375
- mlp_gain: bfloat16 [768], P('dp'), may hold values from 0.099609375 to 1.8984375
- w_qkv: bfloat16 [768, 2304], P('dp'), may hold values from -0.21875 to 0.21875
- w_out: bfloat16 [768, 768], P('dp'), may hold values from -6 to 6
- w_in: bfloat16 [768, 2304], P('dp'), may hold values from -0.21875 to 0.21875
- w_mlp_out: bfloat16 [1152, 768], P('dp'), may hold values from -0.1875 to 0.1875
- block_offsets: int32 [4, 8], P('dp', 'ctx'), may hold values from 0 to 3584, as said below
Outputs:
- mixed: bfloat16 [4, 4096, 768], P('dp', 'ctx')
- tokens_grad: float32 [4, 4096, 768], P('dp', 'ctx')
- attn_gain_grad: float32 [768], P('dp')
- mlp_gain_grad: float32 [768], P('dp')
- w_qkv_grad: float32 [768, 2304], P('dp')
- w_out_grad: float32 [768, 768], P('dp')
- w_in_grad: float32 [768, 2304], P('dp')
- w_mlp_out_grad: float32 [1152, 768], P('dp')
Inputs may be any that keep to these rules, and one draw needn't show every extreme that they name: `block_offsets`: each row holds every multiple of 512 below 4096 exactly once.
All inputs are finite; a program needn't handle non-finite values.
Results may differ from a plain program's by a relative error of at most 0.022.
Values may be sent and summed in bfloat16 or wider, within the bound.
No kernel may reach another device: no remote copies, remote signals or barrier semaphores. Data moves between devices by JAX's collectives and lax.ppermute only.
A program may use at most 128 MiB of HBM per device.

v0:
```python
import jax
import jax.numpy as jnp
from jax import lax
from jax.sharding import PartitionSpec as P

HEADS = 12
HEAD_DIM = 64
FF = 1152
rope_base = 160000.0
norm_eps = 1e-05


def passed_along(x, axis, by):
    count = lax.axis_size(axis)
    return lax.ppermute(x, axis, [(i, (i + by) % count) for i in range(count)])


def layer_norm(values, gain):
    center = values - jnp.mean(values, axis=-1, keepdims=True)
    spread = jnp.mean(center * center, axis=-1, keepdims=True)
    return center * lax.rsqrt(spread + norm_eps) * gain


def norm_back(values, gain, upstream):
    _, pull = jax.vjp(layer_norm, values, gain)
    return pull(upstream)


def rotary_tables(positions, half_size):
    frequency = rope_base ** (-jnp.arange(half_size, dtype=jnp.float32) / half_size)
    angles = positions[:, None] * frequency[None, :]
    cosine = jnp.cos(angles)
    sine_table = jnp.sin(angles)
    return (jnp.concatenate([cosine, cosine], -1), jnp.concatenate([sine_table, sine_table], -1))


def rotate(values, cosine, sine_table):
    half_size = values.shape[-1] // 2
    turned = jnp.concatenate([-values[..., half_size:], values[..., :half_size]], -1)
    return values * cosine[:, None, :] + turned * sine_table[:, None, :]


def unrotate(upstream, cosine, sine_table):
    half_size = upstream.shape[-1] // 2
    turned = upstream * sine_table[:, None, :]
    return upstream * cosine[:, None, :] + jnp.concatenate(
        [turned[..., half_size:], -turned[..., :half_size]], -1
    )


def geglu(packed, hidden_size):
    return jax.nn.gelu(packed[:, :hidden_size], approximate=False) * packed[:, hidden_size:]


def product(left, right):
    return jnp.dot(left, right, preferred_element_type=jnp.float32)


def transposed_left(left, right):
    return lax.dot_general(
        left, right, (((0,), (0,)), ((), ())), preferred_element_type=jnp.float32
    )


def transposed_right(left, right):
    return lax.dot_general(
        left, right, (((1,), (1,)), ((), ())), preferred_element_type=jnp.float32
    )


def key_block():
    return 512


def body(tokens, cotangent, attn_gain, mlp_gain, w_qkv, w_out, w_in, w_mlp_out, block_offsets):
    head_count = HEADS
    head_size = HEAD_DIM
    hidden_size = FF
    model_width = head_count * head_size
    scale = head_size ** (-0.5)
    inputs = tokens[0].astype(jnp.float32)
    row_count = inputs.shape[0]
    positions = (block_offsets[0, 0] + jnp.arange(row_count, dtype=jnp.int32)).astype(jnp.float32)
    cosine, sine_table = rotary_tables(positions, head_size // 2)
    gain_one, gain_two, weight_qkv, weight_out, weight_in, weight_down = (
        lax.all_gather(attn_gain, "dp", axis=0, tiled=True),
        lax.all_gather(mlp_gain, "dp", axis=0, tiled=True),
        lax.all_gather(w_qkv, "dp", axis=0, tiled=True),
        lax.all_gather(w_out, "dp", axis=0, tiled=True),
        lax.all_gather(w_in, "dp", axis=0, tiled=True),
        lax.all_gather(w_mlp_out, "dp", axis=0, tiled=True),
    )
    first_gain = gain_one.astype(jnp.float32)
    second_gain = gain_two.astype(jnp.float32)
    normed = layer_norm(inputs, first_gain).astype(jnp.bfloat16)
    packed = product(normed, weight_qkv).reshape(row_count, 3, head_count, head_size)
    queries = rotate(packed[:, 0], cosine, sine_table).astype(jnp.bfloat16)
    keys_local = (
        rotate(packed[:, 1], cosine, sine_table)
        .astype(jnp.bfloat16)
        .reshape(row_count, model_width)
    )
    values_local = packed[:, 2].astype(jnp.bfloat16).reshape(row_count, model_width)

    def attend(carried, blocks):
        running_max, running_sum, running_out = carried
        key_part, value_part = blocks
        scores = (
            jnp.einsum("qhd,khd->hqk", queries, key_part, preferred_element_type=jnp.float32)
            * scale
        )
        new_max = jnp.maximum(running_max, jnp.max(scores, axis=-1))
        rescale = jnp.exp(running_max - new_max)
        weights = jnp.exp(scores - new_max[:, :, None])
        running_sum = running_sum * rescale + jnp.sum(weights, axis=-1)
        running_out = running_out * rescale.T[:, :, None] + jnp.einsum(
            "hqk,khd->qhd",
            weights.astype(jnp.bfloat16),
            value_part,
            preferred_element_type=jnp.float32,
        )
        return ((new_max, running_sum, running_out), None)

    initial = (
        jnp.full((head_count, row_count), -1e30, jnp.float32),
        jnp.zeros((head_count, row_count), jnp.float32),
        jnp.zeros((row_count, head_count, head_size), jnp.float32),
    )
    carried = initial
    shards = (
        lax.all_gather(keys_local, "ctx", axis=0, tiled=True),
        lax.all_gather(values_local, "ctx", axis=0, tiled=True),
    )
    key_count = shards[0].shape[0]
    block_size = key_block()
    split_keys = shards[0].reshape(key_count // block_size, block_size, head_count, head_size)
    split_values = shards[1].reshape(key_count // block_size, block_size, head_count, head_size)
    carried, _ = lax.scan(attend, carried, (split_keys, split_values))
    running_max, running_sum, running_out = carried
    attended = running_out / running_sum.T[:, :, None]
    log_total = running_max + jnp.log(running_sum)
    attended_low = attended.reshape(row_count, model_width).astype(jnp.bfloat16)
    residual = inputs + product(attended_low, weight_out)
    mlp_normed = layer_norm(residual, second_gain).astype(jnp.bfloat16)
    up_gate = product(mlp_normed, weight_in)
    joined = geglu(up_gate, hidden_size).astype(jnp.bfloat16)
    outputs = residual + product(joined, weight_down)
    mixed = outputs.astype(jnp.bfloat16)[None]
    gain_one, gain_two, weight_qkv, weight_out, weight_in, weight_down = (
        lax.all_gather(attn_gain, "dp", axis=0, tiled=True),
        lax.all_gather(mlp_gain, "dp", axis=0, tiled=True),
        lax.all_gather(w_qkv, "dp", axis=0, tiled=True),
        lax.all_gather(w_out, "dp", axis=0, tiled=True),
        lax.all_gather(w_in, "dp", axis=0, tiled=True),
        lax.all_gather(w_mlp_out, "dp", axis=0, tiled=True),
    )
    first_gain = gain_one.astype(jnp.float32)
    second_gain = gain_two.astype(jnp.float32)
    upstream = cotangent[0].astype(jnp.float32)
    upstream_low = upstream.astype(jnp.bfloat16)
    grad_down = transposed_left(joined, upstream_low)
    grad_joined = transposed_right(upstream_low, weight_down)
    _, glu_pull = jax.vjp(lambda packed_in: geglu(packed_in, hidden_size), up_gate)
    grad_up_gate = glu_pull(grad_joined)[0].astype(jnp.bfloat16)
    grad_in = transposed_left(mlp_normed, grad_up_gate)
    grad_mlp_normed = transposed_right(grad_up_gate, weight_in)
    grad_residual_norm, grad_gain_two = norm_back(residual, second_gain, grad_mlp_normed)
    grad_residual = upstream + grad_residual_norm
    residual_low = grad_residual.astype(jnp.bfloat16)
    grad_out = transposed_left(attended_low, residual_low)
    grad_attended = (
        transposed_right(residual_low, weight_out)
        .astype(jnp.bfloat16)
        .reshape(row_count, head_count, head_size)
    )
    row_delta = jnp.sum(grad_attended.astype(jnp.float32) * attended, axis=-1).T

    def block_grads(query_rows, grad_rows, log_rows, delta_rows, key_rows, value_rows):
        key_count = key_rows.shape[0]
        query_count = query_rows.shape[0]
        block_size = key_block()
        split_keys = key_rows.reshape(key_count // block_size, block_size, head_count, head_size)
        split_values = value_rows.reshape(
            key_count // block_size, block_size, head_count, head_size
        )

        def backward_block(query_grad, blocks):
            key_part, value_part = blocks
            scores = (
                jnp.einsum("qhd,khd->hqk", query_rows, key_part, preferred_element_type=jnp.float32)
                * scale
            )
            probs = jnp.exp(scores - log_rows[:, :, None])
            prob_grad = jnp.einsum(
                "qhd,khd->hqk", grad_rows, value_part, preferred_element_type=jnp.float32
            )
            score_grad = (probs * (prob_grad - delta_rows[:, :, None])).astype(jnp.bfloat16)
            value_grad = jnp.einsum(
                "hqk,qhd->khd",
                probs.astype(jnp.bfloat16),
                grad_rows,
                preferred_element_type=jnp.float32,
            )
            key_grad = (
                jnp.einsum(
                    "hqk,qhd->khd", score_grad, query_rows, preferred_element_type=jnp.float32
                )
                * scale
            )
            query_grad = (
                query_grad
                + jnp.einsum(
                    "hqk,khd->qhd", score_grad, key_part, preferred_element_type=jnp.float32
                )
                * scale
            )
            return (
                query_grad,
                (
                    key_grad.reshape(block_size, model_width),
                    value_grad.reshape(block_size, model_width),
                ),
            )

        query_start = jnp.zeros((query_count, head_count, head_size), jnp.float32)
        query_grad, (key_grad, value_grad) = lax.scan(
            backward_block, query_start, (split_keys, split_values)
        )
        return (
            query_grad,
            key_grad.reshape(key_count, model_width),
            value_grad.reshape(key_count, model_width),
        )

    zero_rows = jnp.zeros((row_count, model_width), jnp.float32)
    zero_heads = jnp.zeros((row_count, head_count, head_size), jnp.float32)

    def cycle_turn(turn_index, carried):
        key_rows, value_rows, key_sum, value_sum, query_sum = carried
        query_add, key_add, value_add = block_grads(
            queries, grad_attended, log_total, row_delta, key_rows, value_rows
        )
        key_sum = key_sum + key_add
        value_sum = value_sum + value_add
        key_rows, value_rows = passed_along((key_rows, value_rows), "ctx", 1)
        key_sum, value_sum = (
            passed_along(key_sum.astype(jnp.bfloat16), "ctx", 1).astype(key_sum.dtype),
            passed_along(value_sum.astype(jnp.bfloat16), "ctx", 1).astype(value_sum.dtype),
        )
        return (key_rows, value_rows, key_sum, value_sum, query_sum + query_add)

    start_state = (keys_local, values_local, zero_rows, zero_rows, zero_heads)
    _, _, grad_keys, grad_values, grad_queries = lax.fori_loop(
        0, lax.axis_size("ctx"), cycle_turn, start_state
    )
    query_back = unrotate(grad_queries, cosine, sine_table).reshape(row_count, model_width)
    key_back = unrotate(
        grad_keys.reshape(row_count, head_count, head_size), cosine, sine_table
    ).reshape(row_count, model_width)
    grad_packed = jnp.concatenate([query_back, key_back, grad_values], axis=1).astype(jnp.bfloat16)
    grad_qkv = transposed_left(normed, grad_packed)
    grad_normed = transposed_right(grad_packed, weight_qkv)
    grad_inputs_norm, grad_gain_one = norm_back(inputs, first_gain, grad_normed)
    tokens_grad = (grad_residual + grad_inputs_norm)[None]
    summed = (
        lax.psum_scatter(
            grad_gain_one.astype(jnp.bfloat16), "dp", scatter_dimension=0, tiled=True
        ).astype(jnp.float32),
        lax.psum_scatter(
            grad_gain_two.astype(jnp.bfloat16), "dp", scatter_dimension=0, tiled=True
        ).astype(jnp.float32),
        lax.psum_scatter(
            grad_qkv.astype(jnp.bfloat16), "dp", scatter_dimension=0, tiled=True
        ).astype(jnp.float32),
        lax.psum_scatter(
            grad_out.astype(jnp.bfloat16), "dp", scatter_dimension=0, tiled=True
        ).astype(jnp.float32),
        lax.psum_scatter(
            grad_in.astype(jnp.bfloat16), "dp", scatter_dimension=0, tiled=True
        ).astype(jnp.float32),
        lax.psum_scatter(
            grad_down.astype(jnp.bfloat16), "dp", scatter_dimension=0, tiled=True
        ).astype(jnp.float32),
    )
    totals = (
        lax.psum(summed[0].astype(jnp.bfloat16), "ctx").astype(jnp.float32),
        lax.psum(summed[1].astype(jnp.bfloat16), "ctx").astype(jnp.float32),
        lax.psum(summed[2].astype(jnp.bfloat16), "ctx").astype(jnp.float32),
        lax.psum(summed[3].astype(jnp.bfloat16), "ctx").astype(jnp.float32),
        lax.psum(summed[4].astype(jnp.bfloat16), "ctx").astype(jnp.float32),
        lax.psum(summed[5].astype(jnp.bfloat16), "ctx").astype(jnp.float32),
    )
    return (mixed, tokens_grad, totals[0], totals[1], totals[2], totals[3], totals[4], totals[5])


def solution(mesh):
    return jax.shard_map(
        body,
        mesh=mesh,
        in_specs=(
            P("dp", "ctx", None),
            P("dp", "ctx", None),
            P("dp"),
            P("dp"),
            P("dp", None),
            P("dp", None),
            P("dp", None),
            P("dp", None),
            P("dp", "ctx"),
        ),
        out_specs=(
            P("dp", "ctx", None),
            P("dp", "ctx", None),
            P("dp"),
            P("dp"),
            P("dp", None),
            P("dp", None),
            P("dp", None),
            P("dp", None),
        ),
        check_vma=False,
    )
```

profile of v0, /device:TPU:0, one launch (start us, length us, event | category | flops | bytes accessed | tf_op | source)
XLA Modules:
  0.0 1304.9 jit_solution(13983983818318694424)
XLA Ops:
  21.6 21.4 %all-gather.7.cloned.1.call-done = bf16[768,2304]{1,0:T(8,128)(2,1)} async-done(((bf16[192,2304]{1,0:T(8,128)(2,1)}), bf16[768,2304]{1,0:T(8,128)(2,1)}) %all-gather.7.cloned.1.call-update) | async-done | bytes 3538960 | tf_op jit(solution)/shard_map/all_gather | solution.py:88
  61.9 95.1 %all-gather.9.cloned.1.call-done = bf16[4096,768]{0,1:T(8,128)(2,1)} async-done(((bf16[512,768]{0,1:T(8,128)(2,1)}), bf16[4096,768]{0,1:T(8,128)(2,1)}) %all-gather.9.cloned.1.call-update) | async-done | bytes 6291472 | tf_op jit(solution)/shard_map/all_gather | solution.py:131
  168.8 87.9 %all-gather.11.cloned.1.call-done = bf16[4096,768]{0,1:T(8,128)(2,1)} async-done(((bf16[512,768]{0,1:T(8,128)(2,1)}), bf16[4096,768]{0,1:T(8,128)(2,1)}) %all-gather.11.cloned.1.call-update) | async-done | bytes 6291472 | tf_op jit(solution)/shard_map/all_gather | solution.py:132
  268.8 145.5 %while.40 = (s32[]{:T(128)}, f32[12,512]{1,0:T(8,128)S(1)}, f32[12,512]{1,0:T(8,128)S(1)}, f32[512,12,64]{0,2,1:T(8,128)S(1)}, bf16[8,512,12,64]{1,3,2,0:T(8,128...) while((s32[]{:T(128)}, f32[12,512]{1,0:T(8,128)S(1)}, ...), condition=%wide.region_5.6_spmd.clone, body=%wide.region_2.5_spmd.clone.sunk | while | flops 831688704 | bytes 93979776 | solution.py:138
  461.1 664.6 %while.41 = (s32[]{:T(128)}, bf16[512,768]{0,1:T(8,128)(2,1)}, bf16[512,768]{0,1:T(8,128)(2,1)}, f32[512,768]{0,1:T(8,128)}, f32[512,768]{0,1:T(8,128)}, /*index...) while((s32[]{:T(128)}, bf16[512,768]{0,1:T(8,128)(2,1)}, ...), condition=%wide.region_12.13_spmd.clone, body=%wide.region_11.12_spmd.clone.sunk | while | flops 2043150336 | bytes 191177200 | solution.py:253
  498.8 15.6 %collective-permute-done.3 = bf16[512,768]{0,1:T(8,128)(2,1)} collective-permute-done((bf16[512,768]{0,1:T(8,128)(2,1)}, bf16[512,768]{0,1:T(8,128)(2,1)}, u32[]{:S(2)}, u32[]{:S(2)}) %collective-permute-start.3) | collective-permute-done | bytes 786464 | tf_op jit(solution)/shard_map/while/body/eval_jaxpr/ppermute | solution.py:15
  516.9 14.3 %collective-permute-done = bf16[512,768]{0,1:T(8,128)(2,1)} collective-permute-done((bf16[512,768]{0,1:T(8,128)(2,1)S(1)}, bf16[512,768]{0,1:T(8,128)(2,1)}, u32[]{:S(2)}, u32[]{:S(2)}) %collective-permute-start) | collective-permute-done | bytes 786464 | tf_op jit(solution)/shard_map/while/body/eval_jaxpr/ppermute | solution.py:15
  531.2 14.9 %collective-permute-done.1 = bf16[512,768]{0,1:T(8,128)(2,1)} collective-permute-done((bf16[512,768]{0,1:T(8,128)(2,1)S(1)}, bf16[512,768]{0,1:T(8,128)(2,1)}, u32[]{:S(2)}, u32[]{:S(2)}) %collective-permute-start.1) | collective-permute-done | bytes 786464 | tf_op jit(solution)/shard_map/while/body/eval_jaxpr/ppermute | solution.py:15
  585.0 15.6 %collective-permute-done.3 = bf16[512,768]{0,1:T(8,128)(2,1)} collective-permute-done((bf16[512,768]{0,1:T(8,128)(2,1)}, bf16[512,768]{0,1:T(8,128)(2,1)}, u32[]{:S(2)}, u32[]{:S(2)}) %collective-permute-start.3) | collective-permute-done | bytes 786464 | tf_op jit(solution)/shard_map/while/body/eval_jaxpr/ppermute | solution.py:15
  603.1 14.4 %collective-permute-done = bf16[512,768]{0,1:T(8,128)(2,1)} collective-permute-done((bf16[512,768]{0,1:T(8,128)(2,1)S(1)}, bf16[512,768]{0,1:T(8,128)(2,1)}, u32[]{:S(2)}, u32[]{:S(2)}) %collective-permute-start) | collective-permute-done | bytes 786464 | tf_op jit(solution)/shard_map/while/body/eval_jaxpr/ppermute | solution.py:15
  617.4 14.0 %collective-permute-done.1 = bf16[512,768]{0,1:T(8,128)(2,1)} collective-permute-done((bf16[512,768]{0,1:T(8,128)(2,1)S(1)}, bf16[512,768]{0,1:T(8,128)(2,1)}, u32[]{:S(2)}, u32[]{:S(2)}) %collective-permute-start.1) | collective-permute-done | bytes 786464 | tf_op jit(solution)/shard_map/while/body/eval_jaxpr/ppermute | solution.py:15
  670.3 15.6 %collective-permute-done.3 = bf16[512,768]{0,1:T(8,128)(2,1)} collective-permute-done((bf16[512,768]{0,1:T(8,128)(2,1)}, bf16[512,768]{0,1:T(8,128)(2,1)}, u32[]{:S(2)}, u32[]{:S(2)}) %collective-permute-start.3) | collective-permute-done | bytes 786464 | tf_op jit(solution)/shard_map/while/body/eval_jaxpr/ppermute | solution.py:15
  688.4 14.4 %collective-permute-done = bf16[512,768]{0,1:T(8,128)(2,1)} collective-permute-done((bf16[512,768]{0,1:T(8,128)(2,1)S(1)}, bf16[512,768]{0,1:T(8,128)(2,1)}, u32[]{:S(2)}, u32[]{:S(2)}) %collective-permute-start) | collective-permute-done | bytes 786464 | tf_op jit(solution)/shard_map/while/body/eval_jaxpr/ppermute | solution.py:15
  702.8 13.1 %collective-permute-done.1 = bf16[512,768]{0,1:T(8,128)(2,1)} collective-permute-done((bf16[512,768]{0,1:T(8,128)(2,1)S(1)}, bf16[512,768]{0,1:T(8,128)(2,1)}, u32[]{:S(2)}, u32[]{:S(2)}) %collective-permute-start.1) | collective-permute-done | bytes 786464 | tf_op jit(solution)/shard_map/while/body/eval_jaxpr/ppermute | solution.py:15
  754.9 15.6 %collective-permute-done.3 = bf16[512,768]{0,1:T(8,128)(2,1)} collective-permute-done((bf16[512,768]{0,1:T(8,128)(2,1)}, bf16[512,768]{0,1:T(8,128)(2,1)}, u32[]{:S(2)}, u32[]{:S(2)}) %collective-permute-start.3) | collective-permute-done | bytes 786464 | tf_op jit(solution)/shard_map/while/body/eval_jaxpr/ppermute | solution.py:15
  772.9 14.4 %collective-permute-done = bf16[512,768]{0,1:T(8,128)(2,1)} collective-permute-done((bf16[512,768]{0,1:T(8,128)(2,1)S(1)}, bf16[512,768]{0,1:T(8,128)(2,1)}, u32[]{:S(2)}, u32[]{:S(2)}) %collective-permute-start) | collective-permute-done | bytes 786464 | tf_op jit(solution)/shard_map/while/body/eval_jaxpr/ppermute | solution.py:15
  787.3 12.3 collective-permute-done.1
  838.5 15.6 %collective-permute-done.3 = bf16[512,768]{0,1:T(8,128)(2,1)} collective-permute-done((bf16[512,768]{0,1:T(8,128)(2,1)}, bf16[512,768]{0,1:T(8,128)(2,1)}, u32[]{:S(2)}, u32[]{:S(2)}) %collective-permute-start.3) | collective-permute-done | bytes 786464 | tf_op jit(solution)/shard_map/while/body/eval_jaxpr/ppermute | solution.py:15
  856.6 14.4 %collective-permute-done = bf16[512,768]{0,1:T(8,128)(2,1)} collective-permute-done((bf16[512,768]{0,1:T(8,128)(2,1)S(1)}, bf16[512,768]{0,1:T(8,128)(2,1)}, u32[]{:S(2)}, u32[]{:S(2)}) %collective-permute-start) | collective-permute-done | bytes 786464 | tf_op jit(solution)/shard_map/while/body/eval_jaxpr/ppermute | solution.py:15
  871.0 11.4 collective-permute-done.1
  910.6 9.3 collective-permute-done.2
  921.3 15.6 %collective-permute-done.3 = bf16[512,768]{0,1:T(8,128)(2,1)} collective-permute-done((bf16[512,768]{0,1:T(8,128)(2,1)}, bf16[512,768]{0,1:T(8,128)(2,1)}, u32[]{:S(2)}, u32[]{:S(2)}) %collective-permute-start.3) | collective-permute-done | bytes 786464 | tf_op jit(solution)/shard_map/while/body/eval_jaxpr/ppermute | solution.py:15
  939.4 14.4 %collective-permute-done = bf16[512,768]{0,1:T(8,128)(2,1)} collective-permute-done((bf16[512,768]{0,1:T(8,128)(2,1)S(1)}, bf16[512,768]{0,1:T(8,128)(2,1)}, u32[]{:S(2)}, u32[]{:S(2)}) %collective-permute-start) | collective-permute-done | bytes 786464 | tf_op jit(solution)/shard_map/while/body/eval_jaxpr/ppermute | solution.py:15
  953.8 10.6 collective-permute-done.1
  1003.2 15.6 %collective-permute-done.3 = bf16[512,768]{0,1:T(8,128)(2,1)} collective-permute-done((bf16[512,768]{0,1:T(8,128)(2,1)}, bf16[512,768]{0,1:T(8,128)(2,1)}, u32[]{:S(2)}, u32[]{:S(2)}) %collective-permute-start.3) | collective-permute-done | bytes 786464 | tf_op jit(solution)/shard_map/while/body/eval_jaxpr/ppermute | solution.py:15
  1021.3 14.4 %collective-permute-done = bf16[512,768]{0,1:T(8,128)(2,1)} collective-permute-done((bf16[512,768]{0,1:T(8,128)(2,1)S(1)}, bf16[512,768]{0,1:T(8,128)(2,1)}, u32[]{:S(2)}, u32[]{:S(2)}) %collective-permute-start) | collective-permute-done | bytes 786464 | tf_op jit(solution)/shard_map/while/body/eval_jaxpr/ppermute | solution.py:15
  1035.7 9.7 collective-permute-done.1
  1084.3 15.6 %collective-permute-done.3 = bf16[512,768]{0,1:T(8,128)(2,1)} collective-permute-done((bf16[512,768]{0,1:T(8,128)(2,1)}, bf16[512,768]{0,1:T(8,128)(2,1)}, u32[]{:S(2)}, u32[]{:S(2)}) %collective-permute-start.3) | collective-permute-done | bytes 786464 | tf_op jit(solution)/shard_map/while/body/eval_jaxpr/ppermute | solution.py:15
  1102.4 14.4 %collective-permute-done = bf16[512,768]{0,1:T(8,128)(2,1)} collective-permute-done((bf16[512,768]{0,1:T(8,128)(2,1)S(1)}, bf16[512,768]{0,1:T(8,128)(2,1)}, u32[]{:S(2)}, u32[]{:S(2)}) %collective-permute-start) | collective-permute-done | bytes 786464 | tf_op jit(solution)/shard_map/while/body/eval_jaxpr/ppermute | solution.py:15
  1138.0 37.4 %reduce-scatter.5.cloned.1.call-done = bf16[192,2304]{1,0:T(8,128)(2,1)} async-done(((bf16[768,2304]{1,0:T(8,128)(2,1)}), bf16[192,2304]{1,0:T(8,128)(2,1)}) %reduce-scatter.5.cloned.1.call-update) | async-done | bytes 884752 | tf_op jit(solution)/shard_map/reduce_scatter | solution.py:272
  1188.3 22.7 %all-reduce.6 = (bf16[192]{0:T(256)(128)(2,1)S(1)}, bf16[192]{0:T(256)(128)(2,1)S(1)}) all-reduce(bf16[192]{0:T(256)(128)(2,1)S(1)} %dynamic-slice.3, bf16[192]{0:T(256)(128)(2,1)S(1)} %dynamic-slice.5), channel_id=1, replica_groups=mesh['ctx'=8,'dp'=4] {'ctx'}, use_global_device_ids=true, to_apply=%region_17.18 | all-reduce | flops 384 | bytes 1536 | tf_op jit(solution)/shard_map/psum | solution.py:286
  1217.6 74.8 %all-reduce.12.cloned.1.call-done = (bf16[192,2304]{1,0:T(8,128)(2,1)}, bf16[192,768]{1,0:T(8,128)(2,1)}, bf16[192,2304]{1,0:T(8,128)(2,1)}, bf16[288,768]{1,0:T(8,128)(2,1)}) async-done(((bf16[192,2304]{1,0:T(8,128)(2,1)}, bf16[192,768]{1,0:T(8,128)(2,1)}, bf16[192,2304]{1,0:T(8,128)(2,1)}, bf16[288,768]{1,0:T(8,128)(2,1)}), (bf16[192,2304]{1,0:T(8,128)(2,1)}, bf16[192,768]{1,0:T(8,128)(2,1)}, ...) | async-done | bytes 2506768 | tf_op jit(solution)/shard_map/psum | solution.py:288
  (497 shorter events, 612.6 us)
Async XLA Ops:
  7.2 35.9 %all-gather.7.cloned.1.call-start = ((), (), s32[]{:S(2)}) async-start(), calls=%async_computation.4 | async-start | bytes 4423680 | tf_op jit(solution)/shard_map/all_gather | solution.py:88
  7.9 149.1 %all-gather.9.cloned.1.call-start = ((), (), s32[]{:S(2)}) async-start(), calls=%async_computation.5 | async-start | bytes 7077888 | tf_op jit(solution)/shard_map/all_gather | solution.py:131
  57.3 199.4 %all-gather.11.cloned.1.call-start = ((), (), s32[]{:S(2)}) async-start(), calls=%async_computation.6 | async-start | bytes 7077888 | tf_op jit(solution)/shard_map/all_gather | solution.py:132
  59.9 355.8 %all-gather.13.cloned.1.call-start = ((), (), s32[]{:S(2)}) async-start(), calls=%async_computation.7 | async-start | bytes 1474560 | tf_op jit(solution)/shard_map/all_gather | solution.py:89
  60.5 359.1 %all-gather.15.cloned.1.call-start = ((), (), s32[]{:S(2)}) async-start(), calls=%async_computation.8 | async-start | bytes 4423680 | tf_op jit(solution)/shard_map/all_gather | solution.py:90
  61.1 365.4 %all-gather.17.cloned.1.call-start = ((), (), s32[]{:S(2)}) async-start(), calls=%async_computation.9 | async-start | bytes 2211840 | tf_op jit(solution)/shard_map/all_gather | solution.py:91
  61.6 1076.3 %reduce-scatter.7.cloned.1.call-start = ((), (), s32[]{:S(2)}) async-start(), calls=%async_computation.11 | async-start | bytes 1474560 | tf_op jit(solution)/shard_map/reduce_scatter | solution.py:275
  446.7 691.2 %reduce-scatter.11.cloned.1.call-start = ((), (), s32[]{:S(2)}) async-start(), calls=%async_computation.13 | async-start | bytes 2211840 | tf_op jit(solution)/shard_map/reduce_scatter | solution.py:281
  449.1 688.9 %reduce-scatter.9.cloned.1.call-start = ((), (), s32[]{:S(2)}) async-start(), calls=%async_computation.12 | async-start | bytes 4423680 | tf_op jit(solution)/shard_map/reduce_scatter | solution.py:278
  461.0 714.4 %reduce-scatter.5.cloned.1.call-start = ((), (), s32[]{:S(2)}) async-start(), calls=%async_computation.10 | async-start | bytes 4423680 | tf_op jit(solution)/shard_map/reduce_scatter | solution.py:272
  483.4 47.8 %collective-permute-start = (bf16[512,768]{0,1:T(8,128)(2,1)S(1)}, bf16[512,768]{0,1:T(8,128)(2,1)}, u32[]{:S(2)}, u32[]{:S(2)}) collective-permute-start(bf16[512,768]{0,1:T(8,128)(2,1)S(1)} %copy.58), channel_id=1, source_target_pairs={{0,4},{4,8},{8,12},{12,16},{16,20},{20,24},{24,28},{28,0},{1,5},{5... | collective-permute-start | bytes 2359304 | tf_op jit(solution)/shard_map/while/body/eval_jaxpr/ppermute | solution.py:15
  483.4 62.7 %collective-permute-start.1 = (bf16[512,768]{0,1:T(8,128)(2,1)S(1)}, bf16[512,768]{0,1:T(8,128)(2,1)}, u32[]{:S(2)}, u32[]{:S(2)}) collective-permute-start(bf16[512,768]{0,1:T(8,128)(2,1)S(1)} %copy-done.6), channel_id=1, source_target_pairs={{0,4},{4,8},{8,12},{12,16},{16,20},{20,24},{24,28},{28,0},{1,5},{5... | collective-permute-start | bytes 2359304 | tf_op jit(solution)/shard_map/while/body/eval_jaxpr/ppermute | solution.py:15
  567.8 32.7 %collective-permute-start.3 = (bf16[512,768]{0,1:T(8,128)(2,1)}, bf16[512,768]{0,1:T(8,128)(2,1)}, u32[]{:S(2)}, u32[]{:S(2)}) collective-permute-start(bf16[512,768]{0,1:T(8,128)(2,1)} %fusion.153), channel_id=1, source_target_pairs={{0,4},{4,8},{8,12},{12,16},{16,20},{20,24},{24,28},{28,0},{1,5},{5... | collective-permute-start | bytes 2359304 | tf_op jit(solution)/shard_map/while/body/eval_jaxpr/ppermute | solution.py:15
  568.8 48.6 %collective-permute-start = (bf16[512,768]{0,1:T(8,128)(2,1)S(1)}, bf16[512,768]{0,1:T(8,128)(2,1)}, u32[]{:S(2)}, u32[]{:S(2)}) collective-permute-start(bf16[512,768]{0,1:T(8,128)(2,1)S(1)} %copy.58), channel_id=1, source_target_pairs={{0,4},{4,8},{8,12},{12,16},{16,20},{20,24},{24,28},{28,0},{1,5},{5... | collective-permute-start | bytes 2359304 | tf_op jit(solution)/shard_map/while/body/eval_jaxpr/ppermute | solution.py:15
  568.9 62.5 %collective-permute-start.1 = (bf16[512,768]{0,1:T(8,128)(2,1)S(1)}, bf16[512,768]{0,1:T(8,128)(2,1)}, u32[]{:S(2)}, u32[]{:S(2)}) collective-permute-start(bf16[512,768]{0,1:T(8,128)(2,1)S(1)} %copy-done.6), channel_id=1, source_target_pairs={{0,4},{4,8},{8,12},{12,16},{16,20},{20,24},{24,28},{28,0},{1,5},{5... | collective-permute-start | bytes 2359304 | tf_op jit(solution)/shard_map/while/body/eval_jaxpr/ppermute | solution.py:15
  653.7 49.1 %collective-permute-start = (bf16[512,768]{0,1:T(8,128)(2,1)S(1)}, bf16[512,768]{0,1:T(8,128)(2,1)}, u32[]{:S(2)}, u32[]{:S(2)}) collective-permute-start(bf16[512,768]{0,1:T(8,128)(2,1)S(1)} %copy.58), channel_id=1, source_target_pairs={{0,4},{4,8},{8,12},{12,16},{16,20},{20,24},{24,28},{28,0},{1,5},{5... | collective-permute-start | bytes 2359304 | tf_op jit(solution)/shard_map/while/body/eval_jaxpr/ppermute | solution.py:15
  653.8 62.1 %collective-permute-start.1 = (bf16[512,768]{0,1:T(8,128)(2,1)S(1)}, bf16[512,768]{0,1:T(8,128)(2,1)}, u32[]{:S(2)}, u32[]{:S(2)}) collective-permute-start(bf16[512,768]{0,1:T(8,128)(2,1)S(1)} %copy-done.6), channel_id=1, source_target_pairs={{0,4},{4,8},{8,12},{12,16},{16,20},{20,24},{24,28},{28,0},{1,5},{5... | collective-permute-start | bytes 2359304 | tf_op jit(solution)/shard_map/while/body/eval_jaxpr/ppermute | solution.py:15
  737.7 32.7 %collective-permute-start.3 = (bf16[512,768]{0,1:T(8,128)(2,1)}, bf16[512,768]{0,1:T(8,128)(2,1)}, u32[]{:S(2)}, u32[]{:S(2)}) collective-permute-start(bf16[512,768]{0,1:T(8,128)(2,1)} %fusion.153), channel_id=1, source_target_pairs={{0,4},{4,8},{8,12},{12,16},{16,20},{20,24},{24,28},{28,0},{1,5},{5... | collective-permute-start | bytes 2359304 | tf_op jit(solution)/shard_map/while/body/eval_jaxpr/ppermute | solution.py:15
  737.8 49.5 %collective-permute-start = (bf16[512,768]{0,1:T(8,128)(2,1)S(1)}, bf16[512,768]{0,1:T(8,128)(2,1)}, u32[]{:S(2)}, u32[]{:S(2)}) collective-permute-start(bf16[512,768]{0,1:T(8,128)(2,1)S(1)} %copy.58), channel_id=1, source_target_pairs={{0,4},{4,8},{8,12},{12,16},{16,20},{20,24},{24,28},{28,0},{1,5},{5... | collective-permute-start | bytes 2359304 | tf_op jit(solution)/shard_map/while/body/eval_jaxpr/ppermute | solution.py:15
  737.9 61.7 %collective-permute-start.1 = (bf16[512,768]{0,1:T(8,128)(2,1)S(1)}, bf16[512,768]{0,1:T(8,128)(2,1)}, u32[]{:S(2)}, u32[]{:S(2)}) collective-permute-start(bf16[512,768]{0,1:T(8,128)(2,1)S(1)} %copy-done.6), channel_id=1, source_target_pairs={{0,4},{4,8},{8,12},{12,16},{16,20},{20,24},{24,28},{28,0},{1,5},{5... | collective-permute-start | bytes 2359304 | tf_op jit(solution)/shard_map/while/body/eval_jaxpr/ppermute | solution.py:15
  821.4 32.7 %collective-permute-start.3 = (bf16[512,768]{0,1:T(8,128)(2,1)}, bf16[512,768]{0,1:T(8,128)(2,1)}, u32[]{:S(2)}, u32[]{:S(2)}) collective-permute-start(bf16[512,768]{0,1:T(8,128)(2,1)} %fusion.153), channel_id=1, source_target_pairs={{0,4},{4,8},{8,12},{12,16},{16,20},{20,24},{24,28},{28,0},{1,5},{5... | collective-permute-start | bytes 2359304 | tf_op jit(solution)/shard_map/while/body/eval_jaxpr/ppermute | solution.py:15
  821.4 49.6 %collective-permute-start = (bf16[512,768]{0,1:T(8,128)(2,1)S(1)}, bf16[512,768]{0,1:T(8,128)(2,1)}, u32[]{:S(2)}, u32[]{:S(2)}) collective-permute-start(bf16[512,768]{0,1:T(8,128)(2,1)S(1)} %copy.58), channel_id=1, source_target_pairs={{0,4},{4,8},{8,12},{12,16},{16,20},{20,24},{24,28},{28,0},{1,5},{5... | collective-permute-start | bytes 2359304 | tf_op jit(solution)/shard_map/while/body/eval_jaxpr/ppermute | solution.py:15
  821.4 61.0 %collective-permute-start.1 = (bf16[512,768]{0,1:T(8,128)(2,1)S(1)}, bf16[512,768]{0,1:T(8,128)(2,1)}, u32[]{:S(2)}, u32[]{:S(2)}) collective-permute-start(bf16[512,768]{0,1:T(8,128)(2,1)S(1)} %copy-done.6), channel_id=1, source_target_pairs={{0,4},{4,8},{8,12},{12,16},{16,20},{20,24},{24,28},{28,0},{1,5},{5... | collective-permute-start | bytes 2359304 | tf_op jit(solution)/shard_map/while/body/eval_jaxpr/ppermute | solution.py:15
  904.2 32.7 %collective-permute-start.3 = (bf16[512,768]{0,1:T(8,128)(2,1)}, bf16[512,768]{0,1:T(8,128)(2,1)}, u32[]{:S(2)}, u32[]{:S(2)}) collective-permute-start(bf16[512,768]{0,1:T(8,128)(2,1)} %fusion.153), channel_id=1, source_target_pairs={{0,4},{4,8},{8,12},{12,16},{16,20},{20,24},{24,28},{28,0},{1,5},{5... | collective-permute-start | bytes 2359304 | tf_op jit(solution)/shard_map/while/body/eval_jaxpr/ppermute | solution.py:15
  904.2 49.6 %collective-permute-start = (bf16[512,768]{0,1:T(8,128)(2,1)S(1)}, bf16[512,768]{0,1:T(8,128)(2,1)}, u32[]{:S(2)}, u32[]{:S(2)}) collective-permute-start(bf16[512,768]{0,1:T(8,128)(2,1)S(1)} %copy.58), channel_id=1, source_target_pairs={{0,4},{4,8},{8,12},{12,16},{16,20},{20,24},{24,28},{28,0},{1,5},{5... | collective-permute-start | bytes 2359304 | tf_op jit(solution)/shard_map/while/body/eval_jaxpr/ppermute | solution.py:15
  904.2 60.2 %collective-permute-start.1 = (bf16[512,768]{0,1:T(8,128)(2,1)S(1)}, bf16[512,768]{0,1:T(8,128)(2,1)}, u32[]{:S(2)}, u32[]{:S(2)}) collective-permute-start(bf16[512,768]{0,1:T(8,128)(2,1)S(1)} %copy-done.6), channel_id=1, source_target_pairs={{0,4},{4,8},{8,12},{12,16},{16,20},{20,24},{24,28},{28,0},{1,5},{5... | collective-permute-start | bytes 2359304 | tf_op jit(solution)/shard_map/while/body/eval_jaxpr/ppermute | solution.py:15
  986.1 49.6 %collective-permute-start = (bf16[512,768]{0,1:T(8,128)(2,1)S(1)}, bf16[512,768]{0,1:T(8,128)(2,1)}, u32[]{:S(2)}, u32[]{:S(2)}) collective-permute-start(bf16[512,768]{0,1:T(8,128)(2,1)S(1)} %copy.58), channel_id=1, source_target_pairs={{0,4},{4,8},{8,12},{12,16},{16,20},{20,24},{24,28},{28,0},{1,5},{5... | collective-permute-start | bytes 2359304 | tf_op jit(solution)/shard_map/while/body/eval_jaxpr/ppermute | solution.py:15
  986.1 59.3 %collective-permute-start.1 = (bf16[512,768]{0,1:T(8,128)(2,1)S(1)}, bf16[512,768]{0,1:T(8,128)(2,1)}, u32[]{:S(2)}, u32[]{:S(2)}) collective-permute-start(bf16[512,768]{0,1:T(8,128)(2,1)S(1)} %copy-done.6), channel_id=1, source_target_pairs={{0,4},{4,8},{8,12},{12,16},{16,20},{20,24},{24,28},{28,0},{1,5},{5... | collective-permute-start | bytes 2359304 | tf_op jit(solution)/shard_map/while/body/eval_jaxpr/ppermute | solution.py:15
  1067.2 32.7 %collective-permute-start.3 = (bf16[512,768]{0,1:T(8,128)(2,1)}, bf16[512,768]{0,1:T(8,128)(2,1)}, u32[]{:S(2)}, u32[]{:S(2)}) collective-permute-start(bf16[512,768]{0,1:T(8,128)(2,1)} %fusion.153), channel_id=1, source_target_pairs={{0,4},{4,8},{8,12},{12,16},{16,20},{20,24},{24,28},{28,0},{1,5},{5... | collective-permute-start | bytes 2359304 | tf_op jit(solution)/shard_map/while/body/eval_jaxpr/ppermute | solution.py:15
  1067.2 49.6 %collective-permute-start = (bf16[512,768]{0,1:T(8,128)(2,1)S(1)}, bf16[512,768]{0,1:T(8,128)(2,1)}, u32[]{:S(2)}, u32[]{:S(2)}) collective-permute-start(bf16[512,768]{0,1:T(8,128)(2,1)S(1)} %copy.58), channel_id=1, source_target_pairs={{0,4},{4,8},{8,12},{12,16},{16,20},{20,24},{24,28},{28,0},{1,5},{5... | collective-permute-start | bytes 2359304 | tf_op jit(solution)/shard_map/while/body/eval_jaxpr/ppermute | solution.py:15
  1067.2 58.4 %collective-permute-start.1 = (bf16[512,768]{0,1:T(8,128)(2,1)S(1)}, bf16[512,768]{0,1:T(8,128)(2,1)}, u32[]{:S(2)}, u32[]{:S(2)}) collective-permute-start(bf16[512,768]{0,1:T(8,128)(2,1)S(1)} %copy-done.6), channel_id=1, source_target_pairs={{0,4},{4,8},{8,12},{12,16},{16,20},{20,24},{24,28},{28,0},{1,5},{5... | collective-permute-start | bytes 2359304 | tf_op jit(solution)/shard_map/while/body/eval_jaxpr/ppermute | solution.py:15
  1137.6 154.8 %all-reduce.12.cloned.1.call-start = ((), (), s32[]{:S(2)}) async-start(), calls=%async_computation.14 | async-start | bytes 5013504 | tf_op jit(solution)/shard_map/psum | solution.py:288
  (119 other events, 1920.9 us)
Sparse Core Ops, SparseCore 0:
  9.5 33.4 all-gather.6
  57.5 99.4 all-gather.8
  159.0 97.6 all-gather.10
  258.1 15.6 all-gather.12
  275.2 30.7 all-gather.14
  307.4 20.7 all-gather.16
  446.8 23.7 reduce-scatter.6
  473.8 29.1 reduce-scatter.10
  505.6 40.3 reduce-scatter.8
  1137.8 37.5 reduce-scatter.4
  1179.3 113.0 all-reduce.11
where the time goes:
time: 1310 us; the launch traced here: 1300 us
  waiting for transfers between devices  720 us (55%)
  matrix products  312 us (24%)
  local copies, waits for them, and re-layouts  107 us (8%)
  other arithmetic  102 us (8%)
  blocking collectives  36.8 us (3%)
  between operations  16.7 us (1%)
    ppermute x32, waiting for transfers between devices, passed_along(): return lax.ppermute(x, axis, [(i, (i + by) % count) for i in range(count)])  401 us
    all_gather x1, waiting for transfers between devices, body(): lax.all_gather(keys_local, 'ctx', axis=0, tiled=True)  95.1 us
    all_gather x1, waiting for transfers between devices, body(): lax.all_gather(values_local, 'ctx', axis=0, tiled=True)  87.9 us
    psum x1, waiting for transfers between devices, body(): lax.psum(summed[2].astype(jnp.bfloat16), 'ctx').astype(jnp.float32)  74.8 us
    dot_general x8, matrix products, attend(): jnp.einsum('qhd,khd->hqk', queries, key_part, preferred_element_type=jnp....  59.3 us
    while x152, local copies, waits for them, and re-layouts  56.3 us
    dot_general x8, matrix products, attend(): jnp.einsum('hqk,khd->qhd', weights.astype(jnp.bfloat16), value_part, pref...  50.9 us
    dot_general x8, matrix products, backward_block(): jnp.einsum('hqk,khd->qhd', score_grad, key_part, preferred_element_type=j...  50.8 us
  transfers between devices with their start and end apart: 43, of which 37 were waited for; matrix products, arithmetic and copies ran while one was open for 33% of the time, Pallas kernels for 0%

commit v1 on v0

--- a/solution.py
+++ b/solution.py
@@ -127,10 +127,23 @@
         jnp.zeros((row_count, head_count, head_size), jnp.float32),
     )
     carried = initial
-    shards = (
-        lax.all_gather(keys_local, "ctx", axis=0, tiled=True),
-        lax.all_gather(values_local, "ctx", axis=0, tiled=True),
-    )
+
+    def change_the_tails(work_x):
+        work_now = lax.axis_size("ctx")
+        tall = lax.axis_index("ctx")
+        part_next, finding = (work_now, tall)
+        plain, ready = (work_x, 1)
+        while ready < part_next:
+            arr_out = lax.ppermute(
+                plain, axis_name="ctx", perm=[(rr, rr ^ ready) for rr in range(part_next)]
+            )
+            earlier = jnp.concatenate([plain, arr_out], axis=0)
+            g_now = jnp.concatenate([arr_out, plain], axis=0)
+            plain = jnp.where(finding & ready == 0, earlier, g_now)
+            ready = 2 * ready
+        return plain
+
+    shards = (change_the_tails(keys_local), lax.all_gather(values_local, "ctx", axis=0, tiled=True))
     key_count = shards[0].shape[0]
     block_size = key_block()
     split_keys = shards[0].reshape(key_count // block_size, block_size, head_count, head_size)

time: 1310 us -> 1400 us (1.069)
  waiting for transfers between devices: 720 us -> 789 us
  other arithmetic: 102 us -> 129 us
    ppermute x0 -> x3, waiting for transfers between devices: none -> 250 us  [change_the_tails(): lax.ppermute(plain, axis_name='ctx', perm=[(rr, rr ^ ready) for rr in ran...]
    all_gather x1 -> x0, waiting for transfers between devices: 95.1 us -> none  [body(): lax.all_gather(keys_local, 'ctx', axis=0, tiled=True)]
    all_gather x1, waiting for transfers between devices: 87.9 us -> 0.01 us  [body(): lax.all_gather(values_local, 'ctx', axis=0, tiled=True)]
    select_n x0 -> x3, other arithmetic: none -> 14.4 us  [change_the_tails(): plain = jnp.where(finding & ready == 0, earlier, g_now)]
    unnamed x99 -> x97, local copies, waits for them, and re-layouts: 41.2 us -> 37.7 us
  transfers between devices with their start and end apart: 43 -> 45, of which waited for: 37 -> 38; matrix products, arithmetic and copies ran while one was open for 33% -> 33% of each run, Pallas kernels for 0% -> 0%
where the time goes in v1:
time: 1400 us
  waiting for transfers between devices  789 us (56%)
  matrix products  311 us (22%)
  other arithmetic  129 us (9%)
  local copies, waits for them, and re-layouts  102 us (7%)
  blocking collectives  36.7 us (3%)
  between operations  17.3 us (1%)
    ppermute x32, waiting for transfers between devices, passed_along(): return lax.ppermute(x, axis, [(i, (i + by) % count) for i in range(count)])  405 us
    ppermute x3, waiting for transfers between devices, change_the_tails(): lax.ppermute(plain, axis_name='ctx', perm=[(rr, rr ^ ready) for rr in ran...  250 us
    psum x1, waiting for transfers between devices, body(): lax.psum(summed[2].astype(jnp.bfloat16), 'ctx').astype(jnp.float32)  74.7 us
    dot_general x8, matrix products, attend(): jnp.einsum('qhd,khd->hqk', queries, key_part, preferred_element_type=jnp....  59.4 us
    while x152, local copies, waits for them, and re-layouts  55 us
    dot_general x8, matrix products, backward_block(): jnp.einsum('hqk,khd->qhd', score_grad, key_part, preferred_element_type=j...  50.8 us
    dot_general x8, matrix products, attend(): jnp.einsum('hqk,khd->qhd', weights.astype(jnp.bfloat16), value_part, pref...  50.4 us
    dot_general x8, matrix products, backward_block(): jnp.einsum('hqk,qhd->khd', probs.astype(jnp.bfloat16), grad_rows, preferr...  49.6 us
  transfers between devices with their start and end apart: 45, of which 38 were waited for; matrix products, arithmetic and copies ran while one was open for 33% of the time, Pallas kernels for 0%

profile of v1, /device:TPU:0, one launch (start us, length us, event | category | flops | bytes accessed | tf_op | source)
XLA Modules:
  0.0 1396.2 jit_solution(8143142882791623941)
XLA Ops:
  22.9 20.1 %all-gather.6.cloned.1.call-done = bf16[768,2304]{1,0:T(8,128)(2,1)} async-done(((bf16[192,2304]{1,0:T(8,128)(2,1)}), bf16[768,2304]{1,0:T(8,128)(2,1)}) %all-gather.6.cloned.1.call-update) | async-done | bytes 3538960 | tf_op jit(solution)/shard_map/all_gather | solution.py:88
  65.9 26.8 %collective-permute-done.4 = bf16[512,768]{0,1:T(8,128)(2,1)} collective-permute-done((bf16[512,768]{0,1:T(8,128)(2,1)}, bf16[512,768]{0,1:T(8,128)(2,1)}, u32[]{:S(2)}, u32[]{:S(2)}) %collective-permute-start.4) | collective-permute-done | bytes 786464 | tf_op jit(solution)/shard_map/ppermute | solution.py:137
  96.7 75.9 %collective-permute-done.5 = bf16[1024,768]{0,1:T(8,128)(2,1)} collective-permute-done((bf16[1024,768]{0,1:T(8,128)(2,1)S(1)}, bf16[1024,768]{0,1:T(8,128)(2,1)}, u32[]{:S(2)}, u32[]{:S(2)}) %collective-permute-start.5) | collective-permute-done | bytes 1572896 | tf_op jit(solution)/shard_map/ppermute | solution.py:137
  177.4 147.2 %collective-permute-done.6 = bf16[2048,768]{0,1:T(8,128)(2,1)} collective-permute-done((bf16[2048,768]{0,1:T(8,128)(2,1)}, bf16[2048,768]{0,1:T(8,128)(2,1)}, u32[]{:S(2)}, u32[]{:S(2)}) %collective-permute-start.6) | collective-permute-done | bytes 3145760 | tf_op jit(solution)/shard_map/ppermute | solution.py:137
  353.7 143.8 %while.40 = (s32[]{:T(128)}, f32[12,512]{1,0:T(8,128)S(1)}, f32[12,512]{1,0:T(8,128)S(1)}, f32[512,12,64]{0,2,1:T(8,128)S(1)}, bf16[8,512,12,64]{1,3,2,0:T(8,128...) while((s32[]{:T(128)}, f32[12,512]{1,0:T(8,128)S(1)}, ...), condition=%wide.region_5.6_spmd.clone, body=%wide.region_2.5_spmd.clone.sunk | while | flops 831688704 | bytes 93979776 | solution.py:151
  543.2 673.9 %while.41 = (s32[]{:T(128)}, bf16[512,768]{0,1:T(8,128)(2,1)}, bf16[512,768]{0,1:T(8,128)(2,1)}, f32[512,768]{0,1:T(8,128)}, f32[512,768]{0,1:T(8,128)}, /*index...) while((s32[]{:T(128)}, bf16[512,768]{0,1:T(8,128)(2,1)}, ...), condition=%wide.region_12.13_spmd.clone, body=%wide.region_11.12_spmd.clone.sunk | while | flops 2043150336 | bytes 191177200 | solution.py:266
  582.1 14.4 %collective-permute-done.3 = bf16[512,768]{0,1:T(8,128)(2,1)} collective-permute-done((bf16[512,768]{0,1:T(8,128)(2,1)}, bf16[512,768]{0,1:T(8,128)(2,1)}, u32[]{:S(2)}, u32[]{:S(2)}) %collective-permute-start.3) | collective-permute-done | bytes 786464 | tf_op jit(solution)/shard_map/while/body/eval_jaxpr/ppermute | solution.py:15
  599.0 14.3 %collective-permute-done = bf16[512,768]{0,1:T(8,128)(2,1)} collective-permute-done((bf16[512,768]{0,1:T(8,128)(2,1)S(1)}, bf16[512,768]{0,1:T(8,128)(2,1)}, u32[]{:S(2)}, u32[]{:S(2)}) %collective-permute-start) | collective-permute-done | bytes 786464 | tf_op jit(solution)/shard_map/while/body/eval_jaxpr/ppermute | solution.py:15
  613.3 16.0 %collective-permute-done.1 = bf16[512,768]{0,1:T(8,128)(2,1)} collective-permute-done((bf16[512,768]{0,1:T(8,128)(2,1)S(1)}, bf16[512,768]{0,1:T(8,128)(2,1)}, u32[]{:S(2)}, u32[]{:S(2)}) %collective-permute-start.1) | collective-permute-done | bytes 786464 | tf_op jit(solution)/shard_map/while/body/eval_jaxpr/ppermute | solution.py:15
  669.5 14.4 %collective-permute-done.3 = bf16[512,768]{0,1:T(8,128)(2,1)} collective-permute-done((bf16[512,768]{0,1:T(8,128)(2,1)}, bf16[512,768]{0,1:T(8,128)(2,1)}, u32[]{:S(2)}, u32[]{:S(2)}) %collective-permute-start.3) | collective-permute-done | bytes 786464 | tf_op jit(solution)/shard_map/while/body/eval_jaxpr/ppermute | solution.py:15
  686.4 14.4 %collective-permute-done = bf16[512,768]{0,1:T(8,128)(2,1)} collective-permute-done((bf16[512,768]{0,1:T(8,128)(2,1)S(1)}, bf16[512,768]{0,1:T(8,128)(2,1)}, u32[]{:S(2)}, u32[]{:S(2)}) %collective-permute-start) | collective-permute-done | bytes 786464 | tf_op jit(solution)/shard_map/while/body/eval_jaxpr/ppermute | solution.py:15
  700.7 15.2 %collective-permute-done.1 = bf16[512,768]{0,1:T(8,128)(2,1)} collective-permute-done((bf16[512,768]{0,1:T(8,128)(2,1)S(1)}, bf16[512,768]{0,1:T(8,128)(2,1)}, u32[]{:S(2)}, u32[]{:S(2)}) %collective-permute-start.1) | collective-permute-done | bytes 786464 | tf_op jit(solution)/shard_map/while/body/eval_jaxpr/ppermute | solution.py:15
  756.0 14.4 %collective-permute-done.3 = bf16[512,768]{0,1:T(8,128)(2,1)} collective-permute-done((bf16[512,768]{0,1:T(8,128)(2,1)}, bf16[512,768]{0,1:T(8,128)(2,1)}, u32[]{:S(2)}, u32[]{:S(2)}) %collective-permute-start.3) | collective-permute-done | bytes 786464 | tf_op jit(solution)/shard_map/while/body/eval_jaxpr/ppermute | solution.py:15
  772.9 14.4 %collective-permute-done = bf16[512,768]{0,1:T(8,128)(2,1)} collective-permute-done((bf16[512,768]{0,1:T(8,128)(2,1)S(1)}, bf16[512,768]{0,1:T(8,128)(2,1)}, u32[]{:S(2)}, u32[]{:S(2)}) %collective-permute-start) | collective-permute-done | bytes 786464 | tf_op jit(solution)/shard_map/while/body/eval_jaxpr/ppermute | solution.py:15
  787.3 14.3 %collective-permute-done.1 = bf16[512,768]{0,1:T(8,128)(2,1)} collective-permute-done((bf16[512,768]{0,1:T(8,128)(2,1)S(1)}, bf16[512,768]{0,1:T(8,128)(2,1)}, u32[]{:S(2)}, u32[]{:S(2)}) %collective-permute-start.1) | collective-permute-done | bytes 786464 | tf_op jit(solution)/shard_map/while/body/eval_jaxpr/ppermute | solution.py:15
  841.7 14.4 %collective-permute-done.3 = bf16[512,768]{0,1:T(8,128)(2,1)} collective-permute-done((bf16[512,768]{0,1:T(8,128)(2,1)}, bf16[512,768]{0,1:T(8,128)(2,1)}, u32[]{:S(2)}, u32[]{:S(2)}) %collective-permute-start.3) | collective-permute-done | bytes 786464 | tf_op jit(solution)/shard_map/while/body/eval_jaxpr/ppermute | solution.py:15
  858.6 14.4 %collective-permute-done = bf16[512,768]{0,1:T(8,128)(2,1)} collective-permute-done((bf16[512,768]{0,1:T(8,128)(2,1)S(1)}, bf16[512,768]{0,1:T(8,128)(2,1)}, u32[]{:S(2)}, u32[]{:S(2)}) %collective-permute-start) | collective-permute-done | bytes 786464 | tf_op jit(solution)/shard_map/while/body/eval_jaxpr/ppermute | solution.py:15
  872.9 13.5 collective-permute-done.1
  926.5 14.4 %collective-permute-done.3 = bf16[512,768]{0,1:T(8,128)(2,1)} collective-permute-done((bf16[512,768]{0,1:T(8,128)(2,1)}, bf16[512,768]{0,1:T(8,128)(2,1)}, u32[]{:S(2)}, u32[]{:S(2)}) %collective-permute-start.3) | collective-permute-done | bytes 786464 | tf_op jit(solution)/shard_map/while/body/eval_jaxpr/ppermute | solution.py:15
  943.4 14.4 %collective-permute-done = bf16[512,768]{0,1:T(8,128)(2,1)} collective-permute-done((bf16[512,768]{0,1:T(8,128)(2,1)S(1)}, bf16[512,768]{0,1:T(8,128)(2,1)}, u32[]{:S(2)}, u32[]{:S(2)}) %collective-permute-start) | collective-permute-done | bytes 786464 | tf_op jit(solution)/shard_map/while/body/eval_jaxpr/ppermute | solution.py:15
  957.7 12.6 collective-permute-done.1
  1010.5 14.4 %collective-permute-done.3 = bf16[512,768]{0,1:T(8,128)(2,1)} collective-permute-done((bf16[512,768]{0,1:T(8,128)(2,1)}, bf16[512,768]{0,1:T(8,128)(2,1)}, u32[]{:S(2)}, u32[]{:S(2)}) %collective-permute-start.3) | collective-permute-done | bytes 786464 | tf_op jit(solution)/shard_map/while/body/eval_jaxpr/ppermute | solution.py:15
  1027.3 14.4 %collective-permute-done = bf16[512,768]{0,1:T(8,128)(2,1)} collective-permute-done((bf16[512,768]{0,1:T(8,128)(2,1)S(1)}, bf16[512,768]{0,1:T(8,128)(2,1)}, u32[]{:S(2)}, u32[]{:S(2)}) %collective-permute-start) | collective-permute-done | bytes 786464 | tf_op jit(solution)/shard_map/while/body/eval_jaxpr/ppermute | solution.py:15
  1041.7 11.8 collective-permute-done.1
  1093.6 14.4 %collective-permute-done.3 = bf16[512,768]{0,1:T(8,128)(2,1)} collective-permute-done((bf16[512,768]{0,1:T(8,128)(2,1)}, bf16[512,768]{0,1:T(8,128)(2,1)}, u32[]{:S(2)}, u32[]{:S(2)}) %collective-permute-start.3) | collective-permute-done | bytes 786464 | tf_op jit(solution)/shard_map/while/body/eval_jaxpr/ppermute | solution.py:15
  1110.4 14.4 %collective-permute-done = bf16[512,768]{0,1:T(8,128)(2,1)} collective-permute-done((bf16[512,768]{0,1:T(8,128)(2,1)S(1)}, bf16[512,768]{0,1:T(8,128)(2,1)}, u32[]{:S(2)}, u32[]{:S(2)}) %collective-permute-start) | collective-permute-done | bytes 786464 | tf_op jit(solution)/shard_map/while/body/eval_jaxpr/ppermute | solution.py:15
  1124.8 10.9 collective-permute-done.1
  1175.8 14.4 %collective-permute-done.3 = bf16[512,768]{0,1:T(8,128)(2,1)} collective-permute-done((bf16[512,768]{0,1:T(8,128)(2,1)}, bf16[512,768]{0,1:T(8,128)(2,1)}, u32[]{:S(2)}, u32[]{:S(2)}) %collective-permute-start.3) | collective-permute-done | bytes 786464 | tf_op jit(solution)/shard_map/while/body/eval_jaxpr/ppermute | solution.py:15
  1192.7 14.4 %collective-permute-done = bf16[512,768]{0,1:T(8,128)(2,1)} collective-permute-done((bf16[512,768]{0,1:T(8,128)(2,1)S(1)}, bf16[512,768]{0,1:T(8,128)(2,1)}, u32[]{:S(2)}, u32[]{:S(2)}) %collective-permute-start) | collective-permute-done | bytes 786464 | tf_op jit(solution)/shard_map/while/body/eval_jaxpr/ppermute | solution.py:15
  1228.7 37.6 %reduce-scatter.5.cloned.1.call-done = bf16[192,2304]{1,0:T(8,128)(2,1)} async-done(((bf16[768,2304]{1,0:T(8,128)(2,1)}), bf16[192,2304]{1,0:T(8,128)(2,1)}) %reduce-scatter.5.cloned.1.call-update) | async-done | bytes 884752 | tf_op jit(solution)/shard_map/reduce_scatter | solution.py:285
  1279.1 22.6 %all-reduce.6 = (bf16[192]{0:T(256)(128)(2,1)S(1)}, bf16[192]{0:T(256)(128)(2,1)S(1)}) all-reduce(bf16[192]{0:T(256)(128)(2,1)S(1)} %dynamic-slice.3, bf16[192]{0:T(256)(128)(2,1)S(1)} %dynamic-slice.5), channel_id=1, replica_groups=mesh['ctx'=8,'dp'=4] {'ctx'}, use_global_device_ids=true, to_apply=%region_17.18 | all-reduce | flops 384 | bytes 1536 | tf_op jit(solution)/shard_map/psum | solution.py:299
  1308.4 74.7 %all-reduce.12.cloned.1.call-done = (bf16[192,2304]{1,0:T(8,128)(2,1)}, bf16[192,768]{1,0:T(8,128)(2,1)}, bf16[192,2304]{1,0:T(8,128)(2,1)}, bf16[288,768]{1,0:T(8,128)(2,1)}) async-done(((bf16[192,2304]{1,0:T(8,128)(2,1)}, bf16[192,768]{1,0:T(8,128)(2,1)}, bf16[192,2304]{1,0:T(8,128)(2,1)}, bf16[288,768]{1,0:T(8,128)(2,1)}), (bf16[192,2304]{1,0:T(8,128)(2,1)}, bf16[192,768]{1,0:T(8,128)(2,1)}, ...) | async-done | bytes 2506768 | tf_op jit(solution)/shard_map/psum | solution.py:301
  (501 shorter events, 648.7 us)
Async XLA Ops:
  7.2 35.9 %all-gather.6.cloned.1.call-start = ((), (), s32[]{:S(2)}) async-start(), calls=%async_computation.4 | async-start | bytes 4423680 | tf_op jit(solution)/shard_map/all_gather | solution.py:88
  7.9 333.5 %all-gather.8.cloned.1.call-start = ((), (), s32[]{:S(2)}) async-start(), calls=%async_computation.5 | async-start | bytes 7077888 | tf_op jit(solution)/shard_map/all_gather | solution.py:146
  56.3 442.5 %all-gather.10.cloned.1.call-start = ((), (), s32[]{:S(2)}) async-start(), calls=%async_computation.6 | async-start | bytes 1474560 | tf_op jit(solution)/shard_map/all_gather | solution.py:89
  57.1 445.7 %all-gather.12.cloned.1.call-start = ((), (), s32[]{:S(2)}) async-start(), calls=%async_computation.7 | async-start | bytes 4423680 | tf_op jit(solution)/shard_map/all_gather | solution.py:90
  65.9 443.7 %all-gather.14.cloned.1.call-start = ((), (), s32[]{:S(2)}) async-start(), calls=%async_computation.8 | async-start | bytes 2211840 | tf_op jit(solution)/shard_map/all_gather | solution.py:91
  95.2 77.4 %collective-permute-start.5 = (bf16[1024,768]{0,1:T(8,128)(2,1)S(1)}, bf16[1024,768]{0,1:T(8,128)(2,1)}, u32[]{:S(2)}, u32[]{:S(2)}) collective-permute-start(bf16[1024,768]{0,1:T(8,128)(2,1)S(1)} %maximum_select_fusion.2), channel_id=1, source_target_pairs={{0,8},{4,12},{8,0},{12,4},{16,24},{20,28},{24,16},{28,20},{1,9},{5... | collective-permute-start | bytes 4718600 | tf_op jit(solution)/shard_map/ppermute | solution.py:137
  176.8 147.7 %collective-permute-start.6 = (bf16[2048,768]{0,1:T(8,128)(2,1)}, bf16[2048,768]{0,1:T(8,128)(2,1)}, u32[]{:S(2)}, u32[]{:S(2)}) collective-permute-start(bf16[2048,768]{0,1:T(8,128)(2,1)} %maximum_select_fusion.1), channel_id=1, source_target_pairs={{0,16},{4,20},{8,24},{12,28},{16,0},{20,4},{24,8},{28,12},{1,17},{... | collective-permute-start | bytes 9437192 | tf_op jit(solution)/shard_map/ppermute | solution.py:137
  177.3 1051.4 %reduce-scatter.7.cloned.1.call-start = ((), (), s32[]{:S(2)}) async-start(), calls=%async_computation.10 | async-start | bytes 1474560 | tf_op jit(solution)/shard_map/reduce_scatter | solution.py:288
  529.6 699.1 %reduce-scatter.11.cloned.1.call-start = ((), (), s32[]{:S(2)}) async-start(), calls=%async_computation.12 | async-start | bytes 2211840 | tf_op jit(solution)/shard_map/reduce_scatter | solution.py:294
  532.0 696.7 %reduce-scatter.9.cloned.1.call-start = ((), (), s32[]{:S(2)}) async-start(), calls=%async_computation.11 | async-start | bytes 4423680 | tf_op jit(solution)/shard_map/reduce_scatter | solution.py:291
  543.1 723.2 %reduce-scatter.5.cloned.1.call-start = ((), (), s32[]{:S(2)}) async-start(), calls=%async_computation.9 | async-start | bytes 4423680 | tf_op jit(solution)/shard_map/reduce_scatter | solution.py:285
  563.8 32.7 %collective-permute-start.3 = (bf16[512,768]{0,1:T(8,128)(2,1)}, bf16[512,768]{0,1:T(8,128)(2,1)}, u32[]{:S(2)}, u32[]{:S(2)}) collective-permute-start(bf16[512,768]{0,1:T(8,128)(2,1)} %fusion.153), channel_id=1, source_target_pairs={{0,4},{4,8},{8,12},{12,16},{16,20},{20,24},{24,28},{28,0},{1,5},{5... | collective-permute-start | bytes 2359304 | tf_op jit(solution)/shard_map/while/body/eval_jaxpr/ppermute | solution.py:15
  563.8 49.6 %collective-permute-start = (bf16[512,768]{0,1:T(8,128)(2,1)S(1)}, bf16[512,768]{0,1:T(8,128)(2,1)}, u32[]{:S(2)}, u32[]{:S(2)}) collective-permute-start(bf16[512,768]{0,1:T(8,128)(2,1)S(1)} %copy.58), channel_id=1, source_target_pairs={{0,4},{4,8},{8,12},{12,16},{16,20},{20,24},{24,28},{28,0},{1,5},{5... | collective-permute-start | bytes 2359304 | tf_op jit(solution)/shard_map/while/body/eval_jaxpr/ppermute | solution.py:15
  563.8 65.6 %collective-permute-start.1 = (bf16[512,768]{0,1:T(8,128)(2,1)S(1)}, bf16[512,768]{0,1:T(8,128)(2,1)}, u32[]{:S(2)}, u32[]{:S(2)}) collective-permute-start(bf16[512,768]{0,1:T(8,128)(2,1)S(1)} %copy-done.6), channel_id=1, source_target_pairs={{0,4},{4,8},{8,12},{12,16},{16,20},{20,24},{24,28},{28,0},{1,5},{5... | collective-permute-start | bytes 2359304 | tf_op jit(solution)/shard_map/while/body/eval_jaxpr/ppermute | solution.py:15
  651.2 32.7 %collective-permute-start.3 = (bf16[512,768]{0,1:T(8,128)(2,1)}, bf16[512,768]{0,1:T(8,128)(2,1)}, u32[]{:S(2)}, u32[]{:S(2)}) collective-permute-start(bf16[512,768]{0,1:T(8,128)(2,1)} %fusion.153), channel_id=1, source_target_pairs={{0,4},{4,8},{8,12},{12,16},{16,20},{20,24},{24,28},{28,0},{1,5},{5... | collective-permute-start | bytes 2359304 | tf_op jit(solution)/shard_map/while/body/eval_jaxpr/ppermute | solution.py:15
  651.2 49.6 %collective-permute-start = (bf16[512,768]{0,1:T(8,128)(2,1)S(1)}, bf16[512,768]{0,1:T(8,128)(2,1)}, u32[]{:S(2)}, u32[]{:S(2)}) collective-permute-start(bf16[512,768]{0,1:T(8,128)(2,1)S(1)} %copy.58), channel_id=1, source_target_pairs={{0,4},{4,8},{8,12},{12,16},{16,20},{20,24},{24,28},{28,0},{1,5},{5... | collective-permute-start | bytes 2359304 | tf_op jit(solution)/shard_map/while/body/eval_jaxpr/ppermute | solution.py:15
  651.2 64.7 %collective-permute-start.1 = (bf16[512,768]{0,1:T(8,128)(2,1)S(1)}, bf16[512,768]{0,1:T(8,128)(2,1)}, u32[]{:S(2)}, u32[]{:S(2)}) collective-permute-start(bf16[512,768]{0,1:T(8,128)(2,1)S(1)} %copy-done.6), channel_id=1, source_target_pairs={{0,4},{4,8},{8,12},{12,16},{16,20},{20,24},{24,28},{28,0},{1,5},{5... | collective-permute-start | bytes 2359304 | tf_op jit(solution)/shard_map/while/body/eval_jaxpr/ppermute | solution.py:15
  737.7 32.7 %collective-permute-start.3 = (bf16[512,768]{0,1:T(8,128)(2,1)}, bf16[512,768]{0,1:T(8,128)(2,1)}, u32[]{:S(2)}, u32[]{:S(2)}) collective-permute-start(bf16[512,768]{0,1:T(8,128)(2,1)} %fusion.153), channel_id=1, source_target_pairs={{0,4},{4,8},{8,12},{12,16},{16,20},{20,24},{24,28},{28,0},{1,5},{5... | collective-permute-start | bytes 2359304 | tf_op jit(solution)/shard_map/while/body/eval_jaxpr/ppermute | solution.py:15
  737.7 49.6 %collective-permute-start = (bf16[512,768]{0,1:T(8,128)(2,1)S(1)}, bf16[512,768]{0,1:T(8,128)(2,1)}, u32[]{:S(2)}, u32[]{:S(2)}) collective-permute-start(bf16[512,768]{0,1:T(8,128)(2,1)S(1)} %copy.58), channel_id=1, source_target_pairs={{0,4},{4,8},{8,12},{12,16},{16,20},{20,24},{24,28},{28,0},{1,5},{5... | collective-permute-start | bytes 2359304 | tf_op jit(solution)/shard_map/while/body/eval_jaxpr/ppermute | solution.py:15
  737.7 63.9 %collective-permute-start.1 = (bf16[512,768]{0,1:T(8,128)(2,1)S(1)}, bf16[512,768]{0,1:T(8,128)(2,1)}, u32[]{:S(2)}, u32[]{:S(2)}) collective-permute-start(bf16[512,768]{0,1:T(8,128)(2,1)S(1)} %copy-done.6), channel_id=1, source_target_pairs={{0,4},{4,8},{8,12},{12,16},{16,20},{20,24},{24,28},{28,0},{1,5},{5... | collective-permute-start | bytes 2359304 | tf_op jit(solution)/shard_map/while/body/eval_jaxpr/ppermute | solution.py:15
  823.4 49.6 %collective-permute-start = (bf16[512,768]{0,1:T(8,128)(2,1)S(1)}, bf16[512,768]{0,1:T(8,128)(2,1)}, u32[]{:S(2)}, u32[]{:S(2)}) collective-permute-start(bf16[512,768]{0,1:T(8,128)(2,1)S(1)} %copy.58), channel_id=1, source_target_pairs={{0,4},{4,8},{8,12},{12,16},{16,20},{20,24},{24,28},{28,0},{1,5},{5... | collective-permute-start | bytes 2359304 | tf_op jit(solution)/shard_map/while/body/eval_jaxpr/ppermute | solution.py:15
  823.4 63.0 %collective-permute-start.1 = (bf16[512,768]{0,1:T(8,128)(2,1)S(1)}, bf16[512,768]{0,1:T(8,128)(2,1)}, u32[]{:S(2)}, u32[]{:S(2)}) collective-permute-start(bf16[512,768]{0,1:T(8,128)(2,1)S(1)} %copy-done.6), channel_id=1, source_target_pairs={{0,4},{4,8},{8,12},{12,16},{16,20},{20,24},{24,28},{28,0},{1,5},{5... | collective-permute-start | bytes 2359304 | tf_op jit(solution)/shard_map/while/body/eval_jaxpr/ppermute | solution.py:15
  908.2 49.6 %collective-permute-start = (bf16[512,768]{0,1:T(8,128)(2,1)S(1)}, bf16[512,768]{0,1:T(8,128)(2,1)}, u32[]{:S(2)}, u32[]{:S(2)}) collective-permute-start(bf16[512,768]{0,1:T(8,128)(2,1)S(1)} %copy.58), channel_id=1, source_target_pairs={{0,4},{4,8},{8,12},{12,16},{16,20},{20,24},{24,28},{28,0},{1,5},{5... | collective-permute-start | bytes 2359304 | tf_op jit(solution)/shard_map/while/body/eval_jaxpr/ppermute | solution.py:15
  908.2 62.2 %collective-permute-start.1 = (bf16[512,768]{0,1:T(8,128)(2,1)S(1)}, bf16[512,768]{0,1:T(8,128)(2,1)}, u32[]{:S(2)}, u32[]{:S(2)}) collective-permute-start(bf16[512,768]{0,1:T(8,128)(2,1)S(1)} %copy-done.6), channel_id=1, source_target_pairs={{0,4},{4,8},{8,12},{12,16},{16,20},{20,24},{24,28},{28,0},{1,5},{5... | collective-permute-start | bytes 2359304 | tf_op jit(solution)/shard_map/while/body/eval_jaxpr/ppermute | solution.py:15
  992.1 49.6 %collective-permute-start = (bf16[512,768]{0,1:T(8,128)(2,1)S(1)}, bf16[512,768]{0,1:T(8,128)(2,1)}, u32[]{:S(2)}, u32[]{:S(2)}) collective-permute-start(bf16[512,768]{0,1:T(8,128)(2,1)S(1)} %copy.58), channel_id=1, source_target_pairs={{0,4},{4,8},{8,12},{12,16},{16,20},{20,24},{24,28},{28,0},{1,5},{5... | collective-permute-start | bytes 2359304 | tf_op jit(solution)/shard_map/while/body/eval_jaxpr/ppermute | solution.py:15
  992.1 61.3 %collective-permute-start.1 = (bf16[512,768]{0,1:T(8,128)(2,1)S(1)}, bf16[512,768]{0,1:T(8,128)(2,1)}, u32[]{:S(2)}, u32[]{:S(2)}) collective-permute-start(bf16[512,768]{0,1:T(8,128)(2,1)S(1)} %copy-done.6), channel_id=1, source_target_pairs={{0,4},{4,8},{8,12},{12,16},{16,20},{20,24},{24,28},{28,0},{1,5},{5... | collective-permute-start | bytes 2359304 | tf_op jit(solution)/shard_map/while/body/eval_jaxpr/ppermute | solution.py:15
  1075.2 32.7 %collective-permute-start.3 = (bf16[512,768]{0,1:T(8,128)(2,1)}, bf16[512,768]{0,1:T(8,128)(2,1)}, u32[]{:S(2)}, u32[]{:S(2)}) collective-permute-start(bf16[512,768]{0,1:T(8,128)(2,1)} %fusion.153), channel_id=1, source_target_pairs={{0,4},{4,8},{8,12},{12,16},{16,20},{20,24},{24,28},{28,0},{1,5},{5... | collective-permute-start | bytes 2359304 | tf_op jit(solution)/shard_map/while/body/eval_jaxpr/ppermute | solution.py:15
  1075.2 49.6 %collective-permute-start = (bf16[512,768]{0,1:T(8,128)(2,1)S(1)}, bf16[512,768]{0,1:T(8,128)(2,1)}, u32[]{:S(2)}, u32[]{:S(2)}) collective-permute-start(bf16[512,768]{0,1:T(8,128)(2,1)S(1)} %copy.58), channel_id=1, source_target_pairs={{0,4},{4,8},{8,12},{12,16},{16,20},{20,24},{24,28},{28,0},{1,5},{5... | collective-permute-start | bytes 2359304 | tf_op jit(solution)/shard_map/while/body/eval_jaxpr/ppermute | solution.py:15
  1075.2 60.5 %collective-permute-start.1 = (bf16[512,768]{0,1:T(8,128)(2,1)S(1)}, bf16[512,768]{0,1:T(8,128)(2,1)}, u32[]{:S(2)}, u32[]{:S(2)}) collective-permute-start(bf16[512,768]{0,1:T(8,128)(2,1)S(1)} %copy-done.6), channel_id=1, source_target_pairs={{0,4},{4,8},{8,12},{12,16},{16,20},{20,24},{24,28},{28,0},{1,5},{5... | collective-permute-start | bytes 2359304 | tf_op jit(solution)/shard_map/while/body/eval_jaxpr/ppermute | solution.py:15
  1157.5 49.6 %collective-permute-start = (bf16[512,768]{0,1:T(8,128)(2,1)S(1)}, bf16[512,768]{0,1:T(8,128)(2,1)}, u32[]{:S(2)}, u32[]{:S(2)}) collective-permute-start(bf16[512,768]{0,1:T(8,128)(2,1)S(1)} %copy.58), channel_id=1, source_target_pairs={{0,4},{4,8},{8,12},{12,16},{16,20},{20,24},{24,28},{28,0},{1,5},{5... | collective-permute-start | bytes 2359304 | tf_op jit(solution)/shard_map/while/body/eval_jaxpr/ppermute | solution.py:15
  1157.5 59.6 %collective-permute-start.1 = (bf16[512,768]{0,1:T(8,128)(2,1)S(1)}, bf16[512,768]{0,1:T(8,128)(2,1)}, u32[]{:S(2)}, u32[]{:S(2)}) collective-permute-start(bf16[512,768]{0,1:T(8,128)(2,1)S(1)} %copy-done.6), channel_id=1, source_target_pairs={{0,4},{4,8},{8,12},{12,16},{16,20},{20,24},{24,28},{28,0},{1,5},{5... | collective-permute-start | bytes 2359304 | tf_op jit(solution)/shard_map/while/body/eval_jaxpr/ppermute | solution.py:15
  1228.3 154.8 %all-reduce.12.cloned.1.call-start = ((), (), s32[]{:S(2)}) async-start(), calls=%async_computation.13 | async-start | bytes 5013504 | tf_op jit(solution)/shard_map/psum | solution.py:301
  (120 other events, 2010.7 us)
Sparse Core Ops, SparseCore 0:
  9.5 33.4 all-gather.5
  56.4 209.0 all-gather.7
  267.1 14.9 all-gather.9
  283.5 30.7 all-gather.11
  315.7 20.7 all-gather.13
  529.7 23.0 reduce-scatter.6
  556.0 29.1 reduce-scatter.10
  587.8 40.3 reduce-scatter.8
  1228.5 37.7 reduce-scatter.4
  1270.0 113.0 all-reduce.11
